TPU v7x, 32 devices: a whole 2x2x4 slice. The times are simulated.
32 devices in a mesh: dp: 4 (over z), seq: 2 (over core), tensor: 4 (over y, x).
Axes of the slice: x: 2, y: 2, z: 4, core: 2. Of those that a mesh axis runs over, the one named last changes fastest.
Arguments:
- block_input: bfloat16 [1024, 1024], P(('dp', 'seq')), may hold values from -6 to 6
- norm1_gain: float32 [1024], replicated, may hold values from 0.5 to 1.5
- q_weight: bfloat16 [1024, 768], replicated, may hold values from -0.1875 to 0.1875
- k_weight: bfloat16 [1024, 768], replicated, may hold values from -0.1875 to 0.1875
- v_weight: bfloat16 [1024, 6, 256], P(None, None, 'tensor'), may hold values from -0.1875 to 0.1875
- gate_weight: bfloat16 [1024, 6, 256], P(None, None, 'tensor'), may hold values from -0.1875 to 0.1875
- beta_weight: bfloat16 [1024, 6], replicated, may hold values from -0.1875 to 0.1875
- decay_weight: bfloat16 [1024, 6], replicated, may hold values from -0.1875 to 0.1875
- q_conv: float32 [4, 768], replicated, may hold values from -3 to 3
- k_conv: float32 [4, 768], replicated, may hold values from -3 to 3
- v_conv: float32 [4, 6, 256], P(None, None, 'tensor'), may hold values from -3 to 3
- decay_scale: float32 [6], replicated, may hold values from 0.0009765625 to 0.05
- dt_bias: float32 [6], replicated, may hold values from -1 to 1
- out_gain: float32 [256], P('tensor'), may hold values from 0.5 to 1.5
- out_weight: bfloat16 [6, 256, 1024], P(None, 'tensor'), may hold values from -0.3125 to 0.3125
- norm2_gain: float32 [1024], replicated, may hold values from 0.5 to 1.5
- ffn_gate: bfloat16 [1024, 2816], P(None, 'tensor'), may hold values from -0.1875 to 0.1875
- ffn_up: bfloat16 [1024, 2816], P(None, 'tensor'), may hold values from -0.1875 to 0.1875
- ffn_down: bfloat16 [2816, 1024], P('tensor'), may hold values from -0.109375 to 0.109375
- cotangent: bfloat16 [1024, 1024], P(('dp', 'seq')), may hold values from -6 to 6
Outputs:
- block_output: bfloat16 [1024, 1024], P(('dp', 'seq'))
- grad_input: float32 [1024, 1024], P(('dp', 'seq'))
- grad_norm1_gain: float32 [1024], replicated
- grad_q_weight: float32 [1024, 768], replicated
- grad_k_weight: float32 [1024, 768], replicated
- grad_v_weight: float32 [1024, 6, 256], P(None, None, 'tensor')
- grad_gate_weight: float32 [1024, 6, 256], P(None, None, 'tensor')
- grad_beta_weight: float32 [1024, 6], replicated
- grad_decay_weight: float32 [1024, 6], replicated
- grad_q_conv: float32 [4, 768], replicated
- grad_k_conv: float32 [4, 768], replicated
- grad_v_conv: float32 [4, 6, 256], P(None, None, 'tensor')
- grad_decay_scale: float32 [6], replicated
- grad_dt_bias: float32 [6], replicated
- grad_out_gain: float32 [256], P('tensor')
- grad_out_weight: float32 [6, 256, 1024], P(None, 'tensor')
- grad_norm2_gain: float32 [1024], replicated
- grad_ffn_gate: float32 [1024, 2816], P(None, 'tensor')
- grad_ffn_up: float32 [1024, 2816], P(None, 'tensor')
- grad_ffn_down: float32 [2816, 1024], P('tensor')
All inputs are finite; a program needn't handle non-finite values.
Results may differ from a plain program's by a relative error of at most 0.025.
Values may be sent and summed in bfloat16 or wider, within the bound.
No kernel may reach another device: no remote copies, remote signals or barrier semaphores. Data moves between devices by JAX's collectives and lax.ppermute only.
A program may use at most 128 MiB of HBM per device.

v0:
```python
import jax
import jax.numpy as jnp
from jax import lax
from jax.sharding import PartitionSpec as P

DV = 256
SPAN = 64
EPS = 1e-06
HIGH_PRECISION = lax.Precision.HIGHEST


def from_behind(value, axis, by):
    length = lax.axis_size(axis)
    pairs = [(i, i + by) for i in range(length) if 0 <= i + by < length]
    return lax.ppermute(value, axis, pairs)


def matmul(left, right):
    return jnp.dot(left, right, preferred_element_type=jnp.float32)


def rms_scale(matrix, gain):
    return matrix * lax.rsqrt(jnp.mean(matrix * matrix, axis=-1, keepdims=True) + EPS) * gain


def swiglu(gate_act, up_act):
    return jax.nn.silu(gate_act) * up_act


def conv_silu(edge_rows, rows, conv_taps):
    length = rows.shape[0]
    padded = jnp.concatenate([edge_rows, rows], axis=0)
    summed = conv_taps[0] * padded[0:length]
    for offset in range(1, conv_taps.shape[0]):
        summed = summed + conv_taps[offset] * padded[offset : offset + length]
    return jax.nn.silu(summed)


def unit_rows(matrix):
    return matrix * lax.rsqrt(jnp.sum(matrix * matrix, axis=-1, keepdims=True) + EPS)


def mixer_inputs(
    q_proj,
    k_proj,
    v_proj,
    b_proj,
    a_proj,
    q_edge,
    k_edge,
    v_edge,
    q_conv,
    k_conv,
    v_conv,
    decay_scale,
    dt_bias,
):
    length = q_proj.shape[0]
    n_heads = b_proj.shape[1]
    queries = conv_silu(q_edge, q_proj, q_conv).reshape(length, n_heads, -1)
    key_vecs = conv_silu(k_edge, k_proj, k_conv).reshape(length, n_heads, -1)
    values = conv_silu(v_edge, v_proj, v_conv.reshape(v_conv.shape[0], -1)).reshape(
        length, n_heads, -1
    )
    queries = unit_rows(queries) * queries.shape[2] ** (-0.5)
    key_vecs = unit_rows(key_vecs)
    beta_gate = jax.nn.sigmoid(b_proj)
    log_decay = -decay_scale * jax.nn.softplus(a_proj + dt_bias)
    return (
        jnp.transpose(queries, (1, 0, 2)),
        jnp.transpose(key_vecs, (1, 0, 2)),
        jnp.transpose(values, (1, 0, 2)),
        beta_gate.T,
        log_decay.T,
    )


def gated_norm(head_out, gate_proj, gain, sum_squares):
    scale_rows = lax.rsqrt(sum_squares / DV + EPS)[..., None]
    return head_out * scale_rows * gain * jax.nn.silu(gate_proj)


def delta_run(queries, key_vecs, values, beta_gate, log_decay, start_state):
    n_heads, length, key_width = key_vecs.shape
    val_width = values.shape[2]
    n_blocks = length // SPAN
    q_blk = queries.reshape(n_heads, n_blocks, SPAN, key_width)
    k_blk = key_vecs.reshape(n_heads, n_blocks, SPAN, key_width)
    v_blk = values.reshape(n_heads, n_blocks, SPAN, val_width)
    b_blk = beta_gate.reshape(n_heads, n_blocks, SPAN)
    g_cum = jnp.cumsum(log_decay.reshape(n_heads, n_blocks, SPAN), axis=-1)
    places = jnp.arange(SPAN)
    strict = places[:, None] > places[None, :]
    within = places[:, None] >= places[None, :]
    differ = g_cum[..., :, None] - g_cum[..., None, :]
    decays = jnp.where(within, jnp.exp(jnp.where(within, differ, 0.0)), 0.0)
    k_gram = jnp.einsum("hnik,hnjk->hnij", k_blk, k_blk, precision=HIGH_PRECISION)
    l_mat = jnp.eye(SPAN, dtype=jnp.float32) + jnp.where(
        strict, b_blk[..., :, None] * k_gram * decays, 0.0
    )
    right_side = jnp.concatenate(
        [b_blk[..., None] * v_blk, (b_blk * jnp.exp(g_cum))[..., None] * k_blk], axis=-1
    )
    solved = lax.linalg.triangular_solve(
        l_mat, right_side, left_side=True, lower=True, unit_diagonal=True
    )
    updates = solved[..., :val_width]
    w_mat = solved[..., val_width:]
    qk_mat = jnp.einsum("hnik,hnjk->hnij", q_blk, k_blk, precision=HIGH_PRECISION) * decays
    g_last = g_cum[..., -1:]
    k_end = k_blk * jnp.exp(g_last - g_cum)[..., None]
    q_dec = q_blk * jnp.exp(g_cum)[..., None]

    def advance(current_state, block_in):
        (
            current_update_rows,
            current_write_rows,
            current_query_decayed,
            current_query_key,
            current_key_edge,
            current_gate_log,
        ) = block_in
        fresh_value_rows = current_update_rows - jnp.einsum(
            "nsz,nzu->nsu", current_write_rows, current_state, precision=HIGH_PRECISION
        )
        block_result = jnp.einsum(
            "nsz,nzu->nsu", current_query_decayed, current_state, precision=HIGH_PRECISION
        ) + jnp.einsum(
            "zdn,znb->zdb", current_query_key, fresh_value_rows, precision=HIGH_PRECISION
        )
        following_state = jnp.exp(current_gate_log)[..., None] * current_state + jnp.einsum(
            "ozq,ozp->oqp", current_key_edge, fresh_value_rows, precision=HIGH_PRECISION
        )
        return (following_state, block_result)

    blocks_in = tuple(
        (jnp.moveaxis(member, 1, 0) for member in (updates, w_mat, q_dec, qk_mat, k_end, g_last))
    )
    final_state, outputs = lax.scan(advance, start_state, blocks_in)
    return (jnp.moveaxis(outputs, 0, 1).reshape(n_heads, length, val_width), final_state)


def on_device(
    block_input,
    norm1_gain,
    q_weight,
    k_weight,
    v_weight,
    gate_weight,
    beta_weight,
    decay_weight,
    q_conv,
    k_conv,
    v_conv,
    decay_scale,
    dt_bias,
    out_gain,
    out_weight,
    norm2_gain,
    ffn_gate,
    ffn_up,
    ffn_down,
    cotangent,
):
    length = block_input.shape[0]
    model_width = block_input.shape[1]
    n_heads = beta_weight.shape[1]
    qk_cols = q_weight.shape[1]
    key_width = qk_cols // n_heads
    value_part = v_weight.shape[2]
    edge_count = q_conv.shape[0] - 1
    inputs_f = block_input.astype(jnp.float32)
    normed1, pull_norm1 = jax.vjp(rms_scale, inputs_f, norm1_gain)
    normed1_b = normed1.astype(jnp.bfloat16)
    v_mat = v_weight.reshape(model_width, -1)
    g_mat = gate_weight.reshape(model_width, -1)
    q_proj = matmul(normed1_b, q_weight)
    k_proj = matmul(normed1_b, k_weight)
    v_proj = matmul(normed1_b, v_mat)
    gate_proj = matmul(normed1_b, g_mat).reshape(length, n_heads, value_part)
    b_proj = matmul(normed1_b, beta_weight)
    a_proj = matmul(normed1_b, decay_weight)
    tail_rows = jnp.concatenate(
        [
            q_proj[length - edge_count :],
            k_proj[length - edge_count :],
            v_proj[length - edge_count :],
        ],
        axis=1,
    )
    edge_rows = from_behind(tail_rows, "seq", 1)
    prepared, pull_inputs = jax.vjp(
        mixer_inputs,
        q_proj,
        k_proj,
        v_proj,
        b_proj,
        a_proj,
        edge_rows[:, :qk_cols],
        edge_rows[:, qk_cols : 2 * qk_cols],
        edge_rows[:, 2 * qk_cols :],
        q_conv,
        k_conv,
        v_conv,
        decay_scale,
        dt_bias,
    )
    queries, key_vecs, values, beta_gate, log_decay = prepared
    empty_state = jnp.zeros((n_heads, key_width, value_part), jnp.float32)
    start_state = empty_state
    unused, end_state = delta_run(queries, key_vecs, values, beta_gate, log_decay, start_state)
    start_state = from_behind(end_state.astype(jnp.bfloat16), "seq", 1).astype(end_state.dtype)
    (mixed_heads, final_state), pull_delta = jax.vjp(
        delta_run, queries, key_vecs, values, beta_gate, log_decay, start_state
    )
    head_out = jnp.transpose(mixed_heads, (1, 0, 2))
    sum_squares = lax.psum(jnp.sum(head_out * head_out, axis=2), "tensor")
    gated, pull_gate = jax.vjp(gated_norm, head_out, gate_proj, out_gain, sum_squares)
    gated_b = gated.astype(jnp.bfloat16).reshape(length, -1)
    o_mat = out_weight.reshape(-1, model_width)
    mixer_total = lax.psum(matmul(gated_b, o_mat).astype(jnp.bfloat16), "tensor").astype(
        jnp.float32
    )
    hidden_res = inputs_f + mixer_total
    normed2, pull_norm2 = jax.vjp(rms_scale, hidden_res, norm2_gain)
    normed2_b = normed2.astype(jnp.bfloat16)
    inner, pull_ffn = jax.vjp(swiglu, matmul(normed2_b, ffn_gate), matmul(normed2_b, ffn_up))
    inner_b = inner.astype(jnp.bfloat16)
    ffn_total = lax.psum(matmul(inner_b, ffn_down).astype(jnp.bfloat16), "tensor").astype(
        jnp.float32
    )
    block_output = (hidden_res + ffn_total).astype(jnp.bfloat16)
    grad_inner = matmul(cotangent, ffn_down.T)
    grad_down = matmul(inner_b.T, cotangent)
    grad_gate_act, grad_up_act = pull_ffn(grad_inner)
    gate_grad_b = grad_gate_act.astype(jnp.bfloat16)
    up_grad_b = grad_up_act.astype(jnp.bfloat16)
    grad_ffn_gate = matmul(normed2_b.T, gate_grad_b)
    grad_ffn_up = matmul(normed2_b.T, up_grad_b)
    normed2_part = matmul(gate_grad_b, ffn_gate.T) + matmul(up_grad_b, ffn_up.T)
    grad_normed2 = lax.psum(normed2_part.astype(jnp.bfloat16), "tensor").astype(jnp.float32)
    grad_hidden_n, grad_norm2 = pull_norm2(grad_normed2)
    grad_hidden = cotangent.astype(jnp.float32) + grad_hidden_n
    grad_hidden_b = grad_hidden.astype(jnp.bfloat16)
    grad_gated = matmul(grad_hidden_b, o_mat.T).reshape(length, n_heads, value_part)
    grad_out_weight = matmul(gated_b.T, grad_hidden_b).reshape(out_weight.shape)
    heads_local, grad_gate_proj, grad_out_gain, squares_local = pull_gate(grad_gated)
    grad_squares = lax.psum(squares_local, "tensor")
    grad_heads = heads_local + 2.0 * head_out * grad_squares[..., None]
    grad_mixed = jnp.transpose(grad_heads, (1, 0, 2))
    end_grad = empty_state
    hop_terms = pull_delta((grad_mixed, end_grad))
    end_grad = from_behind(hop_terms[5].astype(jnp.bfloat16), "seq", -1).astype(jnp.float32)
    full_terms = pull_delta((grad_mixed, end_grad))
    delta_grads = tuple((full_terms[member] for member in range(5)))
    input_grads = pull_inputs(delta_grads)
    edge_grads = jnp.concatenate([input_grads[5], input_grads[6], input_grads[7]], axis=1)
    edge_back = from_behind(edge_grads, "seq", -1)
    q_grad_rows = input_grads[0].at[length - edge_count :].add(edge_back[:, :qk_cols])
    k_grad_rows = input_grads[1].at[length - edge_count :].add(edge_back[:, qk_cols : 2 * qk_cols])
    v_grad_rows = input_grads[2].at[length - edge_count :].add(edge_back[:, 2 * qk_cols :])
    qg_b = q_grad_rows.astype(jnp.bfloat16)
    kg_b = k_grad_rows.astype(jnp.bfloat16)
    vg_b = v_grad_rows.astype(jnp.bfloat16)
    bg_b = input_grads[3].astype(jnp.bfloat16)
    ag_b = input_grads[4].astype(jnp.bfloat16)
    gg_b = grad_gate_proj.reshape(length, -1).astype(jnp.bfloat16)
    normed1_part = (
        matmul(qg_b, q_weight.T)
        + matmul(kg_b, k_weight.T)
        + matmul(vg_b, v_mat.T)
        + matmul(gg_b, g_mat.T)
        + matmul(bg_b, beta_weight.T)
        + matmul(ag_b, decay_weight.T)
    )
    grad_input_n, grad_norm1 = pull_norm1(normed1_part)
    grad_input = grad_hidden + lax.psum(grad_input_n.astype(jnp.bfloat16), "tensor").astype(
        jnp.float32
    )
    shared = lax.psum(
        (
            grad_norm1,
            matmul(normed1_b.T, qg_b),
            matmul(normed1_b.T, kg_b),
            matmul(normed1_b.T, bg_b),
            matmul(normed1_b.T, ag_b),
            input_grads[8],
            input_grads[9],
            input_grads[11],
            input_grads[12],
        ),
        ("dp", "seq", "tensor"),
    )
    value_grad = matmul(normed1_b.T, vg_b).reshape(v_weight.shape)
    gate_grad = matmul(normed1_b.T, gg_b).reshape(gate_weight.shape)
    split = (
        lax.psum(value_grad.astype(jnp.bfloat16), ("dp", "seq")).astype(jnp.float32),
        lax.psum(gate_grad.astype(jnp.bfloat16), ("dp", "seq")).astype(jnp.float32),
        lax.psum(input_grads[10].astype(jnp.bfloat16), ("dp", "seq")).astype(jnp.float32),
        lax.psum(grad_out_gain.astype(jnp.bfloat16), ("dp", "seq")).astype(jnp.float32),
        lax.psum(grad_out_weight.astype(jnp.bfloat16), ("dp", "seq")).astype(jnp.float32),
        lax.psum(grad_norm2.astype(jnp.bfloat16), ("dp", "seq")).astype(jnp.float32),
        lax.psum(grad_ffn_gate.astype(jnp.bfloat16), ("dp", "seq")).astype(jnp.float32),
        lax.psum(grad_ffn_up.astype(jnp.bfloat16), ("dp", "seq")).astype(jnp.float32),
        lax.psum(grad_down.astype(jnp.bfloat16), ("dp", "seq")).astype(jnp.float32),
    )
    return (
        block_output,
        grad_input,
        shared[0],
        shared[1],
        shared[2],
        split[0],
        split[1],
        shared[3],
        shared[4],
        shared[5],
        shared[6],
        split[2],
        shared[7],
        shared[8],
        split[3],
        split[4],
        split[5],
        split[6],
        split[7],
        split[8],
    )


def solution(mesh):
    placed = (
        P(("dp", "seq"), None),
        P(),
        P(),
        P(),
        P(None, None, "tensor"),
        P(None, None, "tensor"),
        P(),
        P(),
        P(),
        P(),
        P(None, None, "tensor"),
        P(),
        P(),
        P("tensor"),
        P(None, "tensor", None),
        P(),
        P(None, "tensor"),
        P(None, "tensor"),
        P("tensor", None),
        P(("dp", "seq"), None),
    )
    return jax.shard_map(
        on_device,
        mesh=mesh,
        in_specs=placed,
        out_specs=(
            P(("dp", "seq"), None),
            P(("dp", "seq"), None),
            P(),
            P(),
            P(),
            P(None, None, "tensor"),
            P(None, None, "tensor"),
            P(),
            P(),
            P(),
            P(),
            P(None, None, "tensor"),
            P(),
            P(),
            P("tensor"),
            P(None, "tensor", None),
            P(),
            P(None, "tensor"),
            P(None, "tensor"),
            P("tensor", None),
        ),
        check_vma=False,
    )
```

profile of v0, /device:TPU:0, one launch (start us, length us, event | category | flops | bytes accessed | tf_op | source)
XLA Modules:
  0.0 872.2 jit_solution(6370596105471412092)
XLA Ops:
  13.4 2.4 collective-permute-start
  16.8 1.4 reduce_window_sum.24
  27.3 59.7 %custom-call.11 = f32[6,2,1,64,64]{3,4,2,1,0:T(8,128)S(1)} custom-call(f32[6,2,1,64,64]{4,3,2,1,0:T(8,128)} %get-tuple-element.1082), custom_call_target="InvertDiagBlocksLowerTriangular" | custom-call | tf_op jit(solution)/shard_map/triangular_solve/custom-call.1 | solution.py:104
  88.1 2.0 fusion.103
  91.2 2.0 while.77
  93.8 1.9 collective-permute-start.1
  95.8 2.7 fusion.145
  101.2 1.9 copy.179
  103.2 2.7 bitcast_multiply_fusion.11
  109.3 9.7 %while.75 = (s32[]{:T(128)}, f32[6,128,64]{1,2,0:T(8,128)S(1)}, f32[2,6,64,64]{3,2,1,0:T(8,128)}, f32[2,6,128,64]{2,3,1,0:T(8,128)}, f32[2,6,64,64]{3,2,1,0:T(8,...) while((s32[]{:T(128)}, f32[6,128,64]{1,2,0:T(8,128)S(1)}, ...), condition=%wide.region_7.9_spmd, body=%wide.region_6.8_spmd.sunk | while | flops 132268032 | bytes 5707657 | solution.py:139
  119.6 1.9 copy.188
  122.8 10.7 %psum.168 = f32[128,6]{0,1:T(8,128)S(1)} all-reduce(f32[128,6]{0,1:T(8,128)S(1)} %fusion.174), channel_id=1, replica_groups=mesh['dp'=4,'seq'=2,'tensor'=4] {'tensor'}, use_global_device_ids=true, to_apply=%region_9.11 | all-reduce | flops 768 | bytes 6144 | tf_op jit(solution)/shard_map/psum | solution.py:217
  134.7 2.2 multiply_convert_fusion.3
  138.5 1.9 copy.193
  140.4 40.1 %all-reduce.39.cloned.1.call-done = bf16[128,1024]{1,0:T(8,128)(2,1)} async-done(((bf16[128,1024]{1,0:T(8,128)(2,1)}), bf16[128,1024]{1,0:T(8,128)(2,1)}) %all-reduce.39.cloned.1.call-update) | async-done | bytes 262160 | tf_op jit(solution)/shard_map/psum | solution.py:221
  182.9 2.0 fusion.242
  187.3 1.6 convolution_convert_fusion.1
  190.0 1.6 convolution_convert_fusion
  192.8 2.7 convolution_convert_fusion.2
  195.5 40.5 %all-reduce.41.cloned.1.call-done = bf16[128,1024]{1,0:T(8,128)(2,1)} async-done(((bf16[128,1024]{1,0:T(8,128)(2,1)}), bf16[128,1024]{1,0:T(8,128)(2,1)}) %all-reduce.41.cloned.1.call-update) | async-done | bytes 262160 | tf_op jit(solution)/shard_map/psum | solution.py:241
  236.0 1.9 fusion.120
  240.0 1.7 multiply_reduce_fusion.14
  242.3 8.9 %psum.172 = f32[128,6]{0,1:T(8,128)S(1)} all-reduce(f32[128,6]{0,1:T(8,128)S(1)} %get-tuple-element.1089), channel_id=1, replica_groups=mesh['dp'=4,'seq'=2,'tensor'=4] {'tensor'}, use_global_device_ids=true, to_apply=%region_16.18 | all-reduce | flops 768 | bytes 6144 | tf_op jit(solution)/shard_map/psum | solution.py:248
  254.3 8.5 while.78
  264.2 2.3 convolution_bitcast_fusion.4
  270.4 20.2 %while.76 = (s32[]{:T(128)}, f32[6,128,64]{1,2,0:T(8,128)S(1)}, f32[2,6,64,64]{3,2,1,0:T(8,128)}, f32[2,6,64,128]{3,2,1,0:T(8,128)}, f32[2,6,64,128]{3,2,0,1:T(8...) while((s32[]{:T(128)}, f32[6,128,64]{1,2,0:T(8,128)S(1)}, ...), condition=%wide.region_21.23_spmd, body=%wide.region_19.22_spmd.sunk | while | flops 264560640 | bytes 16820268 | solution.py:139
  271.6 2.0 fusion.394
  277.6 1.6 fusion.392
  281.6 1.9 fusion.394
  287.6 1.6 fusion.392
  291.2 2.3 fusion.111
  295.9 2.4 multiply_reduce_fusion.10
  299.4 1.4 convolution_add_fusion.14
  302.8 1.5 add_add_fusion.2
  304.3 2.0 copy.214
  306.2 1.7 convolution_add_fusion.17
  310.0 1.8 add_add_fusion.3
  313.0 2.6 multiply_reduce_fusion.3
  321.8 2.1 multiply_reduce_fusion.17
  327.5 1.8 fusion.229
  333.4 1.5 add_add_fusion.4
  336.9 4.0 reduce_window_sum.25
  341.0 2.1 fusion.231
  344.4 1.7 split.35
  346.0 1.7 split.32
  349.1 1.5 scatter-add.11
  350.6 2.4 fusion.247
  354.3 2.6 convolution_add_fusion.13
  359.1 1.8 fusion.94
  371.1 2.3 fusion.248
  373.4 2.3 fusion.246
  376.5 30.4 %all-reduce.29 = (bf16[4,6,64]{2,1,0:T(8,128)(2,1)S(1)}, bf16[64]{0:T(256)(128)(2,1)S(1)}, bf16[1024]{0:T(1024)(128)(2,1)S(1)}) all-reduce(bf16[4,6,64]{2,1,0:T(8,128)(2,1)S(1)} %convert_element_type.192, bf16[64]{0:T(256)(128)(2,1)S(1)} %copy-done.180, ...), channel_id=1, replica_groups=mesh['dp'=4,'seq'=2,'tensor'=4] {'dp','seq'}, use_global_device_ids=true, to_apply=%region_57.59 | all-reduce | flops 2624 | bytes 10496 | tf_op jit(solution)/shard_map/psum | solution.py:299
  408.6 1.4 all-reduce.49.cloned.1.call-done
  410.0 1.8 add_convert_fusion
  411.8 1.8 convert_add_fusion.1
  413.6 144.4 %all-reduce.47.cloned.1.call-done = (bf16[1024,6,64]{0,2,1:T(8,128)(2,1)}, bf16[1024,6,64]{0,2,1:T(8,128)(2,1)}, bf16[6,64,1024]{2,1,0:T(8,128)(2,1)}, bf16[1024...) async-done(((bf16[1024,6,64]{0,2,1:T(8,128)(2,1)}, bf16[1024,6,64]{0,2,1:T(8,128)(2,1)}, bf16[6,64,1024]{2,1,0:T(8,128)(2,1)}, ...) | async-done | bytes 6684688 | tf_op jit(solution)/shard_map/psum | solution.py:297
  558.1 2.5 convert_element_type.187
  563.8 1.9 convert_element_type.201
  565.8 1.9 convert_element_type.203
  567.7 1.9 convert_element_type.205
  569.7 121.7 %all-reduce.43.cloned.1.call-done = (f32[1024]{0:T(1024)}, f32[1024,6]{0,1:T(8,128)}, f32[1024,6]{0,1:T(8,128)}, f32[4,768]{1,0:T(4,128)}, f32[4,768]{1,0:T(4,128)}, /*index=5*/f32[6]{0:T(128)}, f32[6]{0:T(128)}) async-done(((f32[1024]{0:T(1024)}, f32[1024,6]{0,1:T(8,128)}, f32[1024,6]{0,1:T(8,128)}, f32[4,768]{1,0:T(4,128)}, f32[4,768]{1,0:T(4,128)}, /*index=5*/f32[6]{0:T(128)}, f32[6]{0:T(128)}), ...) | async-done | bytes 77888 | tf_op jit(solution)/shard_map/psum | solution.py:280
  691.4 163.4 %all-reduce.45.cloned.1.call-done = (f32[1024,768]{1,0:T(8,128)}, f32[1024,768]{1,0:T(8,128)}) async-done(((f32[1024,768]{1,0:T(8,128)}, f32[1024,768]{1,0:T(8,128)}), (f32[1024,768]{1,0:T(8,128)}, f32[1024,768]{1,0:T(8,128)})) %all-reduce.45.cloned.1.call-update) | async-done | bytes 6291472 | tf_op jit(solution)/shard_map/psum | solution.py:280
  856.1 3.9 copy.411
  860.0 1.7 copy.412
  (645 shorter events, 130.8 us)
Async XLA Ops:
  7.2 173.3 %all-reduce.39.cloned.1.call-start = ((), (), s32[]{:S(2)}) async-start(), calls=%async_computation | async-start | bytes 524288 | tf_op jit(solution)/shard_map/psum | solution.py:221
  10.6 7.7 copy-start.1
  11.0 10.9 %copy-start.39 = (f32[128,768]{1,0:T(8,128)}, f32[128,768]{1,0:T(8,128)S(1)}, u32[]{:S(2)}) copy-start(f32[128,768]{1,0:T(8,128)S(1)} %fusion.239) | copy-start | bytes 1179652
  11.0 4.8 copy-start.183
  11.1 4.9 copy-start.147
  11.1 4.9 copy-start.184
  11.5 13.4 %copy-start.70 = (f32[128,384]{1,0:T(8,128)}, f32[128,384]{1,0:T(8,128)S(1)}, u32[]{:S(2)}) copy-start(f32[128,384]{1,0:T(8,128)S(1)} %fusion.240) | copy-start | bytes 589828
  11.5 6.8 copy-start.104
  11.5 7.3 copy-start.159
  11.5 7.4 copy-start.160
  12.3 6.7 copy-start.161
  13.4 7.9 collective-permute-start
  18.5 5.4 copy-start.130
  18.6 7.5 copy-start.91
  18.8 5.1 copy-start.120
  18.8 5.1 copy-start.122
  18.8 5.1 copy-start.124
  18.9 5.1 copy-start.126
  19.0 7.2 copy-start.100
  20.3 5.8 copy-start.102
  26.1 61.9 %copy-start.45 = (f32[6,128,64]{2,1,0:T(8,128)}, f32[6,128,64]{2,1,0:T(8,128)S(1)}, u32[]{:S(2)}) copy-start(f32[6,128,64]{2,1,0:T(8,128)S(1)} %copy.172) | copy-start | bytes 589828
  91.1 4.6 copy-start.98
  91.1 4.6 copy-start.112
  91.2 4.6 copy-start.114
  91.2 4.6 copy-start.116
  91.2 4.6 copy-start.118
  93.8 13.0 %collective-permute-start.1 = (bf16[6,128,64]{1,2,0:T(8,128)(2,1)}, bf16[6,128,64]{1,2,0:T(8,128)(2,1)}, u32[]{:S(2)}, u32[]{:S(2)}) collective-permute-start(bf16[6,128,64]{1,2,0:T(8,128)(2,1)} %convert_element_type.159), channel_id=1, source_target_pairs={{0,4},{1,5},{2,6},{3,7},{8,12},{9,13},{10,14},{11,15},{16,20},{17,... | collective-permute-start | bytes 294920 | tf_op jit(solution)/shard_map/ppermute | solution.py:15
  99.7 6.2 copy-start.10
  119.0 15.7 %copy-start.2 = (bf16[128,1024]{1,0:T(8,128)(2,1)S(1)}, bf16[128,1024]{1,0:T(8,128)(2,1)}, u32[]{:S(2)}) copy-start(bf16[128,1024]{1,0:T(8,128)(2,1)} %copy-done.1) | copy-start | bytes 786436
  119.0 15.7 %copy-start.181 = (f32[64]{0:T(128)S(1)}, f32[64]{0:T(128)}, u32[]{:S(2)}) copy-start(f32[64]{0:T(128)} %param.49) | copy-start | bytes 772
  136.9 46.0 %copy-start.87 = (bf16[128,6,64]{0,2,1:T(8,128)(2,1)}, bf16[128,6,64]{0,2,1:T(8,128)(2,1)S(1)}, u32[]{:S(2)}) copy-start(bf16[128,6,64]{0,2,1:T(8,128)(2,1)S(1)} %get-tuple-element.1094) | copy-start | bytes 294916
  136.9 43.6 %copy-start.4 = (bf16[128,1024]{1,0:T(8,128)(2,1)S(1)}, bf16[128,1024]{1,0:T(8,128)(2,1)}, u32[]{:S(2)}) copy-start(bf16[128,1024]{1,0:T(8,128)(2,1)} %param.36) | copy-start | bytes 786436
  136.9 44.9 %copy-start.110 = (f32[1024]{0:T(1024)S(1)}, f32[1024]{0:T(1024)}, u32[]{:S(2)}) copy-start(f32[1024]{0:T(1024)} %param.51) | copy-start | bytes 12292
  138.0 98.0 %all-reduce.41.cloned.1.call-start = ((), (), s32[]{:S(2)}) async-start(), calls=%async_computation.1 | async-start | bytes 524288 | tf_op jit(solution)/shard_map/psum | solution.py:241
  180.5 4.4 copy-start.34
  192.7 217.3 %all-reduce.49.cloned.1.call-start = ((), (), s32[]{:S(2)}) async-start(), calls=%async_computation.5 | async-start | bytes 1048576 | tf_op jit(solution)/shard_map/psum | solution.py:229
  236.0 4.1 copy-start.174
  236.0 4.1 copy-start.182
  239.3 12.0 %copy-start.95 = (f32[128,6,64]{0,2,1:T(8,128)S(1)}, f32[128,6,64]{0,2,1:T(8,128)}, u32[]{:S(2)}) copy-start(f32[128,6,64]{0,2,1:T(8,128)} %get-tuple-element.1095) | copy-start | bytes 589828
  254.3 9.9 %copy-start.89 = (bf16[128,6,64]{0,2,1:T(8,128)(2,1)S(1)}, bf16[128,6,64]{0,2,1:T(8,128)(2,1)}, u32[]{:S(2)}) copy-start(bf16[128,6,64]{0,2,1:T(8,128)(2,1)} %get-tuple-element.1055) | copy-start | bytes 294916
  262.9 3.6 collective-permute-start.2
  270.4 4.9 copy-start.6
  270.5 4.9 copy-start.54
  280.5 4.9 copy-start.6
  280.5 4.9 copy-start.54
  304.3 4.6 copy-start.11
  308.8 4.1 copy-start.40
  308.8 4.1 copy-start.42
  321.8 7.4 copy-start.97
  321.8 7.4 copy-start.108
  321.8 11.6 %copy-start.93 = (f32[6,2,64]{2,1,0:T(2,128)S(1)}, f32[6,2,64]{2,1,0:T(2,128)}, u32[]{:S(2)}) copy-start(f32[6,2,64]{2,1,0:T(2,128)} %copy-done.91) | copy-start | bytes 9220
  324.7 23.6 %copy-start.19 = (f32[128,768]{1,0:T(8,128)S(1)}, f32[128,768]{1,0:T(8,128)}, u32[]{:S(2)}) copy-start(f32[128,768]{1,0:T(8,128)} %copy-done.18) | copy-start | bytes 1179652
  324.7 23.6 %copy-start.21 = (f32[128,768]{1,0:T(8,128)S(1)}, f32[128,768]{1,0:T(8,128)}, u32[]{:S(2)}) copy-start(f32[128,768]{1,0:T(8,128)} %copy-done.20) | copy-start | bytes 1179652
  326.2 22.2 %collective-permute-start.3 = (f32[3,1920]{1,0:T(4,128)}, f32[3,1920]{1,0:T(4,128)}, u32[]{:S(2)}, u32[]{:S(2)}) collective-permute-start(f32[3,1920]{1,0:T(4,128)} %pad_maximum_fusion.4), channel_id=1, source_target_pairs={{4,0},{5,1},{6,2},{7,3},{12,8},{13,9},{14,10},{15,11},{20,16},{21,... | collective-permute-start | bytes 69128 | tf_op jit(solution)/shard_map/ppermute | solution.py:15
  341.0 7.4 copy-start.23
  341.0 7.4 copy-start.25
  341.0 7.4 copy-start.27
  349.1 5.2 copy-start.29
  363.1 194.9 %all-reduce.47.cloned.1.call-start = ((), (), s32[]{:S(2)}) async-start(), calls=%async_computation.4 | async-start | bytes 13369344 | tf_op jit(solution)/shard_map/psum | solution.py:297
  367.1 324.3 %all-reduce.43.cloned.1.call-start = ((), (), s32[]{:S(2)}) async-start(), calls=%async_computation.2 | async-start | bytes 190464 | tf_op jit(solution)/shard_map/psum | solution.py:280
  373.4 481.5 %all-reduce.45.cloned.1.call-start = ((), (), s32[]{:S(2)}) async-start(), calls=%async_computation.3 | async-start | bytes 12582912 | tf_op jit(solution)/shard_map/psum | solution.py:280
  375.7 34.3 %copy-start.17 = (bf16[128,1024]{1,0:T(8,128)(2,1)S(1)}, bf16[128,1024]{1,0:T(8,128)(2,1)}, u32[]{:S(2)}) copy-start(bf16[128,1024]{1,0:T(8,128)(2,1)} %all-reduce.39.cloned.1.call-done) | copy-start | bytes 786436
  860.0 4.1 copy-start.186
  860.0 4.6 copy-start.185
  (152 other events, 338.9 us)
Sparse Core Ops, SparseCore 0:
  138.1 42.4 all-reduce.38
  192.9 43.0 all-reduce.40
  363.2 46.7 all-reduce.48
  414.5 143.5 all-reduce.46
  565.5 125.8 all-reduce.42
  697.6 157.1 all-reduce.44
where the time goes:
time: 883 us; the launch traced here: 872 us
  waiting for transfers between devices  512 us (58%)
  other arithmetic  132 us (15%)
  matrix products  86.7 us (10%)
  local copies, waits for them, and re-layouts  66.9 us (8%)
  blocking collectives  50.1 us (6%)
  between operations  16.5 us (2%)
    psum x2, waiting for transfers between devices, on_device(): lax.psum((grad_norm1, matmul(normed1_b.T, qg_b), matmul(normed1_b.T, kg_b...  285 us
    psum x1, waiting for transfers between devices, on_device(): lax.psum(value_grad.astype(jnp.bfloat16), ('dp', 'seq')).astype(jnp.float32)  144 us
    another operation x5, other arithmetic, delta_run(): lax.linalg.triangular_solve(l_mat, right_side, left_side=True, lower=True...  61 us
    psum x1, waiting for transfers between devices, on_device(): lax.psum(normed2_part.astype(jnp.bfloat16), 'tensor').astype(jnp.float32)  40.5 us
    psum x1, waiting for transfers between devices, on_device(): lax.psum(matmul(gated_b, o_mat).astype(jnp.bfloat16), 'tensor')  40.1 us
    dot_general x30, matrix products, matmul(): return jnp.dot(left, right, preferred_element_type=jnp.float32)  38.7 us
    psum x1, blocking collectives, on_device(): lax.psum(input_grads[10].astype(jnp.bfloat16), ('dp', 'seq'))  30.4 us
    unnamed x363, local copies, waits for them, and re-layouts  25.5 us
  transfers between devices with their start and end apart: 10, of which 6 were waited for; matrix products, arithmetic and copies ran while one was open for 8% of the time, Pallas kernels for 0%

commit v1 on v0

--- a/solution.py
+++ b/solution.py
@@ -278,18 +278,21 @@
         jnp.float32
     )
     shared = lax.psum(
-        (
-            grad_norm1,
-            matmul(normed1_b.T, qg_b),
-            matmul(normed1_b.T, kg_b),
-            matmul(normed1_b.T, bg_b),
-            matmul(normed1_b.T, ag_b),
-            input_grads[8],
-            input_grads[9],
-            input_grads[11],
-            input_grads[12],
+        lax.psum(
+            (
+                grad_norm1,
+                matmul(normed1_b.T, qg_b),
+                matmul(normed1_b.T, kg_b),
+                matmul(normed1_b.T, bg_b),
+                matmul(normed1_b.T, ag_b),
+                input_grads[8],
+                input_grads[9],
+                input_grads[11],
+                input_grads[12],
+            ),
+            ("seq", "tensor"),
         ),
-        ("dp", "seq", "tensor"),
+        "dp",
     )
     value_grad = matmul(normed1_b.T, vg_b).reshape(v_weight.shape)
     gate_grad = matmul(normed1_b.T, gg_b).reshape(gate_weight.shape)

time: 883 us -> 1020 us (1.16)
  waiting for transfers between devices: 512 us -> 647 us
    psum x0 -> x2, waiting for transfers between devices: none -> 252 us  [on_device(): lax.psum(lax.psum((grad_norm1, matmul(normed1_b.T, qg_b), matmul(normed1_...]
    psum x2, waiting for transfers between devices: 285 us -> 150 us  [on_device(): lax.psum((grad_norm1, matmul(normed1_b.T, qg_b), matmul(normed1_b.T, kg_b...]
    psum x1, waiting for transfers between devices: 1.43 us -> 18.1 us  [on_device(): lax.psum(matmul(inner_b, ffn_down).astype(jnp.bfloat16), 'tensor')]
    unnamed x363 -> x383, local copies, waits for them, and re-layouts: 25.5 us -> 25.3 us
  transfers between devices with their start and end apart: 10 -> 12, of which waited for: 6 -> 8; matrix products, arithmetic and copies ran while one was open for 8% -> 7% of each run, Pallas kernels for 0% -> 0%
where the time goes in v1:
time: 1020 us; the launch traced here: 1010 us
  waiting for transfers between devices  647 us (63%)
  other arithmetic  129 us (13%)
  matrix products  86.2 us (8%)
  local copies, waits for them, and re-layouts  73.1 us (7%)
  blocking collectives  48 us (5%)
  between operations  16.6 us (2%)
    psum x2, waiting for transfers between devices, on_device(): lax.psum(lax.psum((grad_norm1, matmul(normed1_b.T, qg_b), matmul(normed1_...  252 us
    psum x2, waiting for transfers between devices, on_device(): lax.psum((grad_norm1, matmul(normed1_b.T, qg_b), matmul(normed1_b.T, kg_b...  150 us
    psum x1, waiting for transfers between devices, on_device(): lax.psum(value_grad.astype(jnp.bfloat16), ('dp', 'seq')).astype(jnp.float32)  144 us
    another operation x5, other arithmetic, delta_run(): lax.linalg.triangular_solve(l_mat, right_side, left_side=True, lower=True...  61 us
    psum x1, waiting for transfers between devices, on_device(): lax.psum(matmul(gated_b, o_mat).astype(jnp.bfloat16), 'tensor')  42 us
    psum x1, waiting for transfers between devices, on_device(): lax.psum(normed2_part.astype(jnp.bfloat16), 'tensor').astype(jnp.float32)  41.2 us
    dot_general x30, matrix products, matmul(): return jnp.dot(left, right, preferred_element_type=jnp.float32)  37.4 us
    psum x1, blocking collectives, on_device(): lax.psum(input_grads[10].astype(jnp.bfloat16), ('dp', 'seq'))  28.3 us
  transfers between devices with their start and end apart: 12, of which 8 were waited for; matrix products, arithmetic and copies ran while one was open for 7% of the time, Pallas kernels for 0%

profile of v1, /device:TPU:0, one launch (start us, length us, event | category | flops | bytes accessed | tf_op | source)
XLA Modules:
  0.0 1008.5 jit_solution(4679060872180510569)
XLA Ops:
  13.4 2.4 collective-permute-start
  27.4 59.7 %custom-call.11 = f32[6,2,1,64,64]{3,4,2,1,0:T(8,128)S(1)} custom-call(f32[6,2,1,64,64]{4,3,2,1,0:T(8,128)} %get-tuple-element.1091), custom_call_target="InvertDiagBlocksLowerTriangular" | custom-call | tf_op jit(solution)/shard_map/triangular_solve/custom-call.1 | solution.py:104
  88.1 2.1 fusion.103
  91.2 2.0 while.77
  93.9 1.9 collective-permute-start.1
  95.8 2.8 fusion.145
  101.3 1.9 copy.179
  103.2 2.7 bitcast_multiply_fusion.11
  109.3 9.7 while.75
  119.6 1.9 copy.188
  122.8 10.7 %psum.231 = f32[128,6]{0,1:T(8,128)S(1)} all-reduce(f32[128,6]{0,1:T(8,128)S(1)} %fusion.174), channel_id=1, replica_groups=mesh['dp'=4,'seq'=2,'tensor'=4] {'tensor'}, use_global_device_ids=true, to_apply=%region_9.11 | all-reduce | flops 768 | bytes 6144 | tf_op jit(solution)/shard_map/psum | solution.py:217
  134.2 2.3 multiply_convert_fusion.3
  138.6 42.0 %all-reduce.43.cloned.1.call-done = bf16[128,1024]{1,0:T(8,128)(2,1)} async-done(((bf16[128,1024]{1,0:T(8,128)(2,1)}), bf16[128,1024]{1,0:T(8,128)(2,1)}) %all-reduce.43.cloned.1.call-update) | async-done | bytes 262160 | tf_op jit(solution)/shard_map/psum | solution.py:221
  183.0 2.0 fusion.242
  188.8 1.9 copy.193
  190.8 41.2 %all-reduce.45.cloned.1.call-done = bf16[128,1024]{1,0:T(8,128)(2,1)} async-done(((bf16[128,1024]{1,0:T(8,128)(2,1)}), bf16[128,1024]{1,0:T(8,128)(2,1)}) %all-reduce.45.cloned.1.call-update) | async-done | bytes 262160 | tf_op jit(solution)/shard_map/psum | solution.py:241
  231.9 1.9 fusion.120
  236.7 2.4 multiply_reduce_fusion.14
  239.7 8.9 psum.235
  251.7 8.5 while.78
  261.5 2.3 convolution_bitcast_fusion.4
  267.8 20.2 %while.76 = (s32[]{:T(128)}, f32[6,128,64]{1,2,0:T(8,128)S(1)}, f32[2,6,64,64]{3,2,1,0:T(8,128)}, f32[2,6,64,128]{3,2,1,0:T(8,128)}, f32[2,6,64,128]{3,2,0,1:T(8...) while((s32[]{:T(128)}, f32[6,128,64]{1,2,0:T(8,128)S(1)}, ...), condition=%wide.region_21.23_spmd, body=%wide.region_19.22_spmd.sunk | while | flops 264560640 | bytes 16820268 | solution.py:139
  269.0 1.9 fusion.394
  275.0 1.6 fusion.392
  279.0 1.9 fusion.394
  285.0 1.6 fusion.392
  288.6 2.3 fusion.111
  293.3 2.5 multiply_reduce_fusion.10
  298.3 1.9 copy.213
  301.3 1.8 add_add_fusion.2
  303.1 2.0 copy.214
  305.1 2.4 convolution_add_fusion.17
  307.5 1.9 copy.202
  310.6 1.8 add_add_fusion.3
  313.6 3.3 multiply_reduce_fusion.3
  320.4 1.8 copy.216
  322.3 1.7 copy.217
  324.0 1.9 multiply_reduce_fusion.17
  335.0 1.5 add_add_fusion.4
  337.3 4.0 reduce_window_sum.25
  350.3 1.7 split.35
  351.9 1.7 split.32
  357.0 2.4 fusion.247
  359.5 2.3 fusion.248
  361.8 1.4 convolution_add_fusion.13
  366.9 2.3 fusion.246
  370.2 1.6 convolution_convert_fusion.1
  371.8 1.6 convolution_convert_fusion
  374.6 1.6 convolution_convert_fusion.2
  381.0 41.4 %all-reduce.47.cloned.1.call-done = (f32[1024]{0:T(1024)}, f32[1024,6]{0,1:T(8,128)}, f32[1024,6]{0,1:T(8,128)}, f32[4,768]{1,0:T(4,128)}, f32[4,768]{1,0:T(4,128)}, /*index=5*/f32[6]{0:T(128)}, f32[6]{0:T(128)}) async-done(((f32[1024]{0:T(1024)}, f32[1024,6]{0,1:T(8,128)}, f32[1024,6]{0,1:T(8,128)}, f32[4,768]{1,0:T(4,128)}, f32[4,768]{1,0:T(4,128)}, /*index=5*/f32[6]{0:T(128)}, f32[6]{0:T(128)}), ...) | async-done | bytes 77888 | tf_op jit(solution)/shard_map/psum | solution.py:281
  422.5 108.2 %all-reduce.49.cloned.1.call-done = (f32[1024,768]{1,0:T(8,128)}, f32[1024,768]{1,0:T(8,128)}) async-done(((f32[1024,768]{1,0:T(8,128)}, f32[1024,768]{1,0:T(8,128)}), (f32[1024,768]{1,0:T(8,128)}, f32[1024,768]{1,0:T(8,128)})) %all-reduce.49.cloned.1.call-update) | async-done | bytes 6291472 | tf_op jit(solution)/shard_map/psum | solution.py:281
  531.5 28.3 %all-reduce.31 = (bf16[4,6,64]{2,1,0:T(8,128)(2,1)S(1)}, bf16[64]{0:T(256)(128)(2,1)S(1)}, bf16[1024]{0:T(1024)(128)(2,1)S(1)}) all-reduce(bf16[4,6,64]{2,1,0:T(8,128)(2,1)S(1)} %convert_element_type.192, bf16[64]{0:T(256)(128)(2,1)S(1)} %copy-done.191, ...), channel_id=1, replica_groups=mesh['dp'=4,'seq'=2,'tensor'=4] {'dp','seq'}, use_global_device_ids=true, to_apply=%region_64.66 | all-reduce | flops 2624 | bytes 10496 | tf_op jit(solution)/shard_map/psum | solution.py:302
  561.5 18.1 %all-reduce.57.cloned.1.call-done = (bf16[128,1024]{1,0:T(8,128)(2,1)}, bf16[128,1024]{1,0:T(8,128)(2,1)}) async-done(((bf16[128,1024]{1,0:T(8,128)(2,1)}, bf16[128,1024]{1,0:T(8,128)(2,1)}), (bf16[128,1024]{1,0:T(8,128)(2,1)}, bf16[128,1024]{1,0:T(8,128)(2,1)})) %all-reduce.57.cloned.1.call-update) | async-done | bytes 524304 | tf_op jit(solution)/shard_map/psum | solution.py:229
  579.6 1.8 add_convert_fusion
  581.4 1.8 convert_add_fusion.1
  583.2 144.4 %all-reduce.55.cloned.1.call-done = (bf16[1024,6,64]{0,2,1:T(8,128)(2,1)}, bf16[1024,6,64]{0,2,1:T(8,128)(2,1)}, bf16[6,64,1024]{2,1,0:T(8,128)(2,1)}, bf16[1024...) async-done(((bf16[1024,6,64]{0,2,1:T(8,128)(2,1)}, bf16[1024,6,64]{0,2,1:T(8,128)(2,1)}, bf16[6,64,1024]{2,1,0:T(8,128)(2,1)}, ...) | async-done | bytes 6684688 | tf_op jit(solution)/shard_map/psum | solution.py:300
  727.6 2.5 convert_element_type.187
  733.4 1.9 convert_element_type.201
  735.4 1.9 convert_element_type.203
  737.3 1.9 convert_element_type.205
  739.2 26.7 %all-reduce.51.cloned.1.call-done = (f32[1024]{0:T(1024)}, f32[1024,6]{0,1:T(8,128)}, f32[1024,6]{0,1:T(8,128)}, f32[4,768]{1,0:T(4,128)}, f32[4,768]{1,0:T(4,128)}, /*index=5*/f32[6]{0:T(128)}, f32[6]{0:T(128)}) async-done(((f32[1024]{0:T(1024)}, f32[1024,6]{0,1:T(8,128)}, f32[1024,6]{0,1:T(8,128)}, f32[4,768]{1,0:T(4,128)}, f32[4,768]{1,0:T(4,128)}, /*index=5*/f32[6]{0:T(128)}, f32[6]{0:T(128)}), ...) | async-done | bytes 77888 | tf_op jit(solution)/shard_map/psum | solution.py:280
  765.9 225.2 %all-reduce.53.cloned.1.call-done = (f32[1024,768]{1,0:T(8,128)}, f32[1024,768]{1,0:T(8,128)}) async-done(((f32[1024,768]{1,0:T(8,128)}, f32[1024,768]{1,0:T(8,128)}), (f32[1024,768]{1,0:T(8,128)}, f32[1024,768]{1,0:T(8,128)})) %all-reduce.53.cloned.1.call-update) | async-done | bytes 6291472 | tf_op jit(solution)/shard_map/psum | solution.py:280
  992.3 3.9 copy.420
  996.3 1.7 copy.421
  (671 shorter events, 136.0 us)
Async XLA Ops:
  7.2 173.5 %all-reduce.43.cloned.1.call-start = ((), (), s32[]{:S(2)}) async-start(), calls=%async_computation | async-start | bytes 524288 | tf_op jit(solution)/shard_map/psum | solution.py:221
  10.6 7.7 copy-start.1
  11.0 11.0 %copy-start.44 = (f32[128,768]{1,0:T(8,128)}, f32[128,768]{1,0:T(8,128)S(1)}, u32[]{:S(2)}) copy-start(f32[128,768]{1,0:T(8,128)S(1)} %fusion.239) | copy-start | bytes 1179652
  11.1 4.8 copy-start.193
  11.1 4.9 copy-start.166
  11.1 4.9 copy-start.194
  11.5 13.5 %copy-start.77 = (f32[128,384]{1,0:T(8,128)}, f32[128,384]{1,0:T(8,128)S(1)}, u32[]{:S(2)}) copy-start(f32[128,384]{1,0:T(8,128)S(1)} %fusion.240) | copy-start | bytes 589828
  11.5 6.8 copy-start.119
  11.5 7.3 copy-start.170
  11.5 7.4 copy-start.171
  12.3 6.7 copy-start.172
  13.4 7.9 collective-permute-start
  18.5 5.5 copy-start.150
  18.6 7.6 copy-start.106
  18.8 5.1 copy-start.138
  18.8 5.1 copy-start.140
  18.9 5.1 copy-start.142
  18.9 5.1 copy-start.144
  19.0 7.2 copy-start.115
  20.3 5.8 copy-start.117
  26.2 61.9 %copy-start.49 = (f32[6,128,64]{2,1,0:T(8,128)}, f32[6,128,64]{2,1,0:T(8,128)S(1)}, u32[]{:S(2)}) copy-start(f32[6,128,64]{2,1,0:T(8,128)S(1)} %copy.172) | copy-start | bytes 589828
  91.2 4.7 copy-start.111
  91.2 4.6 copy-start.130
  93.9 13.0 %collective-permute-start.1 = (bf16[6,128,64]{1,2,0:T(8,128)(2,1)}, bf16[6,128,64]{1,2,0:T(8,128)(2,1)}, u32[]{:S(2)}, u32[]{:S(2)}) collective-permute-start(bf16[6,128,64]{1,2,0:T(8,128)(2,1)} %convert_element_type.159), channel_id=1, source_target_pairs={{0,4},{1,5},{2,6},{3,7},{8,12},{9,13},{10,14},{11,15},{16,20},{17,... | collective-permute-start | bytes 294920 | tf_op jit(solution)/shard_map/ppermute | solution.py:15
  99.8 6.1 copy-start.11
  119.0 15.1 %copy-start.2 = (bf16[128,1024]{1,0:T(8,128)(2,1)S(1)}, bf16[128,1024]{1,0:T(8,128)(2,1)}, u32[]{:S(2)}) copy-start(bf16[128,1024]{1,0:T(8,128)(2,1)} %copy-done.1) | copy-start | bytes 786436
  119.0 15.1 %copy-start.192 = (f32[64]{0:T(128)S(1)}, f32[64]{0:T(128)}, u32[]{:S(2)}) copy-start(f32[64]{0:T(128)} %param.49) | copy-start | bytes 772
  134.1 46.5 %copy-start.4 = (bf16[128,1024]{1,0:T(8,128)(2,1)S(1)}, bf16[128,1024]{1,0:T(8,128)(2,1)}, u32[]{:S(2)}) copy-start(bf16[128,1024]{1,0:T(8,128)(2,1)} %param.36) | copy-start | bytes 786436
  134.2 47.8 %copy-start.128 = (f32[1024]{0:T(1024)S(1)}, f32[1024]{0:T(1024)}, u32[]{:S(2)}) copy-start(f32[1024]{0:T(1024)} %param.51) | copy-start | bytes 12292
  138.1 93.8 %all-reduce.45.cloned.1.call-start = ((), (), s32[]{:S(2)}) async-start(), calls=%async_computation.1 | async-start | bytes 524288 | tf_op jit(solution)/shard_map/psum | solution.py:241
  187.6 44.3 %copy-start.5 = (bf16[128,1024]{1,0:T(8,128)(2,1)S(1)}, bf16[128,1024]{1,0:T(8,128)(2,1)}, u32[]{:S(2)}) copy-start(bf16[128,1024]{1,0:T(8,128)(2,1)} %param.36) | copy-start | bytes 786436
  188.8 233.6 %all-reduce.47.cloned.1.call-start = ((), (), s32[]{:S(2)}) async-start(), calls=%async_computation.2 | async-start | bytes 190464 | tf_op jit(solution)/shard_map/psum | solution.py:281
  231.9 4.8 copy-start.94
  231.9 4.8 copy-start.108
  235.9 12.7 %copy-start.109 = (f32[128,6,64]{0,2,1:T(8,128)S(1)}, f32[128,6,64]{0,2,1:T(8,128)}, u32[]{:S(2)}) copy-start(f32[128,6,64]{0,2,1:T(8,128)} %get-tuple-element.1104) | copy-start | bytes 589828
  251.6 9.8 copy-start.104
  260.2 3.6 collective-permute-start.2
  267.8 4.9 copy-start.7
  267.8 4.9 copy-start.58
  277.8 4.9 copy-start.7
  277.8 4.9 copy-start.58
  300.2 4.9 copy-start.124
  303.1 6.3 copy-start.12
  305.1 5.5 copy-start.153
  319.6 6.4 copy-start.159
  319.6 6.4 copy-start.161
  319.6 6.4 copy-start.163
  319.6 6.4 copy-start.165
  326.9 10.3 %copy-start.151 = (f32[128,6]{0,1:T(8,128)S(1)}, f32[128,6]{0,1:T(8,128)}, u32[]{:S(2)}) copy-start(f32[128,6]{0,1:T(8,128)} %copy-done.150) | copy-start | bytes 9220
  326.9 14.4 %copy-start.3 = (bf16[128,1024]{1,0:T(8,128)(2,1)S(1)}, bf16[128,1024]{1,0:T(8,128)(2,1)}, u32[]{:S(2)}) copy-start(bf16[128,1024]{1,0:T(8,128)(2,1)} %copy-done.1) | copy-start | bytes 786436
  328.2 26.6 %copy-start.22 = (f32[128,768]{1,0:T(8,128)S(1)}, f32[128,768]{1,0:T(8,128)}, u32[]{:S(2)}) copy-start(f32[128,768]{1,0:T(8,128)} %copy-done.21) | copy-start | bytes 1179652
  328.2 26.6 %copy-start.24 = (f32[128,768]{1,0:T(8,128)S(1)}, f32[128,768]{1,0:T(8,128)}, u32[]{:S(2)}) copy-start(f32[128,768]{1,0:T(8,128)} %copy-done.23) | copy-start | bytes 1179652
  328.8 26.0 %collective-permute-start.3 = (f32[3,1920]{1,0:T(4,128)}, f32[3,1920]{1,0:T(4,128)}, u32[]{:S(2)}, u32[]{:S(2)}) collective-permute-start(f32[3,1920]{1,0:T(4,128)} %pad_maximum_fusion.4), channel_id=1, source_target_pairs={{4,0},{5,1},{6,2},{7,3},{12,8},{13,9},{14,10},{15,11},{20,16},{21,... | collective-permute-start | bytes 69128 | tf_op jit(solution)/shard_map/ppermute | solution.py:15
  341.4 13.4 %copy-start.26 = (f32[128,768]{1,0:T(8,128)S(1)}, f32[128,768]{1,0:T(8,128)}, u32[]{:S(2)}) copy-start(f32[128,768]{1,0:T(8,128)} %copy-done.25) | copy-start | bytes 1179652
  341.4 13.4 %copy-start.28 = (f32[128,768]{1,0:T(8,128)S(1)}, f32[128,768]{1,0:T(8,128)}, u32[]{:S(2)}) copy-start(f32[128,768]{1,0:T(8,128)} %copy-done.27) | copy-start | bytes 1179652
  341.4 13.4 %copy-start.30 = (f32[128,768]{1,0:T(8,128)S(1)}, f32[128,768]{1,0:T(8,128)}, u32[]{:S(2)}) copy-start(f32[128,768]{1,0:T(8,128)} %copy-done.29) | copy-start | bytes 1179652
  341.4 13.4 %copy-start.32 = (f32[128,768]{1,0:T(8,128)S(1)}, f32[128,768]{1,0:T(8,128)}, u32[]{:S(2)}) copy-start(f32[128,768]{1,0:T(8,128)} %copy-done.31) | copy-start | bytes 1179652
  366.9 163.8 %all-reduce.49.cloned.1.call-start = ((), (), s32[]{:S(2)}) async-start(), calls=%async_computation.3 | async-start | bytes 12582912 | tf_op jit(solution)/shard_map/psum | solution.py:281
  369.2 210.4 %all-reduce.57.cloned.1.call-start = ((), (), s32[]{:S(2)}) async-start(), calls=%async_computation.7 | async-start | bytes 1048576 | tf_op jit(solution)/shard_map/psum | solution.py:229
  377.1 350.5 %all-reduce.55.cloned.1.call-start = ((), (), s32[]{:S(2)}) async-start(), calls=%async_computation.6 | async-start | bytes 13369344 | tf_op jit(solution)/shard_map/psum | solution.py:300
  381.0 384.9 %all-reduce.51.cloned.1.call-start = ((), (), s32[]{:S(2)}) async-start(), calls=%async_computation.4 | async-start | bytes 190464 | tf_op jit(solution)/shard_map/psum | solution.py:280
  422.4 568.6 %all-reduce.53.cloned.1.call-start = ((), (), s32[]{:S(2)}) async-start(), calls=%async_computation.5 | async-start | bytes 12582912 | tf_op jit(solution)/shard_map/psum | solution.py:280
  530.7 48.9 %copy-start.18 = (bf16[128,1024]{1,0:T(8,128)(2,1)S(1)}, bf16[128,1024]{1,0:T(8,128)(2,1)}, u32[]{:S(2)}) copy-start(bf16[128,1024]{1,0:T(8,128)(2,1)} %all-reduce.43.cloned.1.call-done) | copy-start | bytes 786436
  996.3 4.6 copy-start.195
  (164 other events, 393.7 us)
Sparse Core Ops, SparseCore 0:
  138.2 42.3 all-reduce.42
  188.9 43.0 all-reduce.44
  367.0 55.3 all-reduce.46
  426.1 104.4 all-reduce.48
  534.1 45.5 all-reduce.56
  584.1 143.5 all-reduce.54
  730.5 35.3 all-reduce.50
  768.3 222.7 all-reduce.52
